TPU v7x, 512 devices: a whole 4x8x8 slice. The times are simulated.
512 devices in a mesh: gx: 8 (over x, core), gy: 8 (over y), obs: 8 (over z).
Axes of the slice: x: 4, y: 8, z: 8, core: 2. Of those that a mesh axis runs over, the one named last changes fastest.
Arguments:
- control: float32 [4, 8, 1024, 1024], P(None, 'obs', 'gy', 'gx'), may hold values from -6 to 6
- diffusivity: float32 [2, 8, 1024, 1024], P(None, 'obs', 'gy', 'gx'), may hold values from 0.12 to 0.245
- prof_tile: int32 [32768, 1], P(('gx', 'gy')), may hold values from 0 to 63; in each aligned block of 512 rows (0 to 511, 512 to 1023, ...) at most 16 rows name the same one
- prof_cell: int32 [32768], P(('gx', 'gy')), may hold values from 0 to 16383
- obs_prof: int32 [262144], P(('gx', 'gy', 'obs')), may hold values from 0 to 511
- obs_field: int32 [262144], P(('gx', 'gy', 'obs')), may hold values from 0 to 3
- obs_level: int32 [262144], P(('gx', 'gy', 'obs')), may hold values from 0 to 6
- obs_weight: float32 [262144], P(('gx', 'gy', 'obs')), may hold values from 0 to 1
- innovation: float32 [262144], P(('gx', 'gy', 'obs')), may hold values from -6 to 6
- obs_precision: float32 [262144], P(('gx', 'gy', 'obs')), may hold values from 0.25 to 4
Outputs:
- gradient: float32 [4, 8, 1024, 1024], P(None, 'obs', 'gy', 'gx')
- departures: float32 [262144], P(('gx', 'gy', 'obs'))
Inputs may be any that keep to these rules, and one draw needn't show every extreme that they name: `prof_tile`: in each aligned block of 512 rows (the profiles of one tile) no tile is named by more than 16 rows; in some blocks one tile is named by exactly 16 rows.
All inputs are finite; a program needn't handle non-finite values.
Results may differ from a plain program's by a relative error of at most 0.00002.
Values sent between devices are 32-bit elements; how exact they have to be, the bound alone decides.
No kernel may reach another device: no remote copies, remote signals or barrier semaphores. Data moves between devices by JAX's collectives and lax.ppermute only.
A program may use at most 64 MiB of HBM per device.

v0:
```python
import jax
import jax.numpy as jnp
from jax import lax
from jax.experimental import pallas as pl
from jax.experimental.pallas import tpu as pltpu
from jax.sharding import PartitionSpec as P


STEPS = 10
HALO = STEPS
ROWS = 16
PITCH = 2 * HALO
PAD = 8
F32, BF16, I32 = jnp.float32, jnp.bfloat16, jnp.int32


def lanes(shape):
    return lax.broadcasted_iota(I32, shape, len(shape) - 1)


def subs(shape):
    return lax.broadcasted_iota(I32, shape, len(shape) - 2)


def split3(x):
    hi = x.astype(BF16)
    rest = x - hi.astype(F32)
    mid = rest.astype(BF16)
    low = (rest - mid.astype(F32)).astype(BF16)
    return hi, mid, low


def one_hot(flags):
    return jnp.where(flags, 1.0, 0.0).astype(BF16)


def dot_nn(a, b):
    return lax.dot_general(a, b, (((1,), (0,)), ((), ())), preferred_element_type=F32)


def dot_nt(a, b):
    return lax.dot_general(a, b, (((1,), (1,)), ((), ())), preferred_element_type=F32)


def call(body, outs, args, scratch=(), flops=1_000_000, hbm=False):
    vmem = pl.BlockSpec(memory_space=pltpu.VMEM)
    given = pl.BlockSpec(memory_space=pltpu.HBM) if hbm else vmem
    outs = [o if isinstance(o, jax.ShapeDtypeStruct) else jax.ShapeDtypeStruct(o, F32) for o in outs]
    return pl.pallas_call(
        body,
        out_shape=outs,
        in_specs=[given] * len(args),
        out_specs=[vmem] * len(outs),
        scratch_shapes=list(scratch),
        cost_estimate=pl.CostEstimate(
            flops=flops,
            bytes_accessed=sum(4 * x.size for x in (*args, *outs)),
            transcendentals=0,
        ),
        compiler_params=pltpu.CompilerParams(vmem_limit_bytes=16 << 20),
    )(*args)


def mask_north(rate_ref):
    last = rate_ref.shape[1] - 8
    rows = rate_ref[1, pl.ds(last, 8), :]
    top = lax.axis_index("gy") == lax.axis_size("gy") - 1
    rate_ref[1, pl.ds(last, 8), :] = jnp.where(top & (subs(rows.shape) == 7), 0.0, rows)


def pack_edges(arrays, east_ref, west_ref):
    lane = lanes(arrays[0].shape)
    east = jnp.zeros(arrays[0].shape, F32)
    west = jnp.zeros(arrays[0].shape, F32)
    for a, x in enumerate(arrays):
        width = x.shape[-1]
        low = a * PITCH + HALO
        moved = pltpu.roll(x, (low - (width - HALO)) % width, 1)
        east = jnp.where((lane >= low) & (lane < low + HALO), moved, east)
        low = a * PITCH
        moved = pltpu.roll(x, low % width, 1) if low else x
        west = jnp.where((lane >= low) & (lane < low + HALO), moved, west)
    east_ref[...] = east
    west_ref[...] = west


def pack_inputs(*refs):
    sources, (east, west, obs), kept, sems = refs[:10], refs[10:13], refs[13:23], refs[23]
    copies = [
        pltpu.make_async_copy(source, target, sems.at[i])
        for i, (source, target) in enumerate(zip(sources, kept))
    ]
    for copy in copies:
        copy.start()
    for copy in copies:
        copy.wait()
    ctl, rate, _, _, prof, field, level, weight, innov, prec = kept
    mask_north(rate)
    pack_edges([ctl[f] for f in range(ctl.shape[0])] + [rate[0], rate[1]], east, west)
    index = ((field[...] * 8 + level[...]) * 512 + prof[...]).astype(F32)
    rows = jnp.concatenate([index, weight[...], innov[...], prec[...]], axis=0)
    for z in range(obs.shape[0] // rows.shape[0]):
        obs[pl.ds(z * rows.shape[0], rows.shape[0]), :] = rows


def north_south(arrays, strip, north_ref, south_ref):
    for a, x in enumerate(arrays + [strip]):
        north_ref[a] = x[x.shape[0] - ROWS :]
        south_ref[a] = x[:ROWS]


def edges_first(ctl, rate, left, right, strip, north, south):
    joined = left[...] + right[...]
    strip[...] = joined
    arrays = [ctl[f] for f in range(ctl.shape[0])] + [rate[0], rate[1]]
    north_south(arrays, joined, north, south)


def edges_second(pulled, left, right, strip, north, south):
    joined = left[...] + right[...]
    strip[...] = joined
    north_south([pulled[f] for f in range(pulled.shape[0])], joined, north, south)


def unpack(block, a):
    width = block.shape[-1]
    east = pltpu.roll(block, (-a * PITCH) % width, 1) if a else block
    west = pltpu.roll(block, (width - HALO - a * PITCH - HALO) % width, 1)
    return jnp.where(lanes(block.shape) < width // 2, east, west)


def blocks(own, south, north):
    height = own.shape[0]
    return ((PAD, south), (PAD + ROWS, own), (PAD + ROWS + height, north))


def turned(main, beyond, by):
    width = main.shape[-1]
    edge = lanes(main.shape) == (0 if by == 1 else width - 1)
    a = pltpu.roll(main, by % width, 1)
    b = pltpu.roll(beyond, by % width, 1)
    return jnp.where(edge, b, a), jnp.where(edge, a, b)


def one_step(source, coef, store, first, last):
    fields = source.shape[0] // 2
    for tile in range(first, last):
        row = PAD + 8 * tile
        here, up, down = pl.ds(row, 8), pl.ds(row + 1, 8), pl.ds(row - 1, 8)
        c = [coef[i, pl.ds(8 * tile, 8), :] for i in range(10)]
        for f in range(fields):
            m, s = source[2 * f, here, :], source[2 * f + 1, here, :]
            me, se = turned(m, s, -1)
            mw, sw = turned(m, s, 1)
            new_m = c[0] * m + c[2] * me + c[4] * mw + c[6] * source[2 * f, up, :]
            new_m = new_m + c[8] * source[2 * f, down, :]
            new_s = c[1] * s + c[3] * se + c[5] * sw + c[7] * source[2 * f + 1, up, :]
            new_s = new_s + c[9] * source[2 * f + 1, down, :]
            store(f, tile, new_m, new_s)


def ten_steps(a, b, coef, finish, tiles):
    def into(target):
        def store(f, tile, main, beyond):
            target[2 * f, pl.ds(PAD + 8 * tile, 8), :] = main
            target[2 * f + 1, pl.ds(PAD + 8 * tile, 8), :] = beyond

        return store

    one_step(a, coef, into(b), 0, tiles)

    def body(_, carry):
        one_step(b, coef, into(a), 1, tiles - 1)
        one_step(a, coef, into(b), 1, tiles - 1)
        return carry

    lax.fori_loop(0, STEPS // 2 - 1, body, 0)

    def store(f, tile, main, beyond):
        finish(f, 8 * tile - ROWS, main)

    one_step(b, coef, store, ROWS // 8, tiles - ROWS // 8)


def load_field(a, own, strip, south, north):
    fields = own.shape[0]
    for f in range(fields):
        for row, block in blocks(own[f], south[f], north[f]):
            a[2 * f, pl.ds(row, block.shape[0]), :] = block
    for row, block in blocks(strip[...], south[south.shape[0] - 1], north[north.shape[0] - 1]):
        for f in range(fields):
            a[2 * f + 1, pl.ds(row, block.shape[0]), :] = unpack(block, f)
    clear = jnp.zeros((PAD, a.shape[2]), F32)
    for plane in range(a.shape[0]):
        a[plane, pl.ds(0, PAD), :] = clear
        a[plane, pl.ds(a.shape[1] - PAD, PAD), :] = clear


def diffuse_control(ctl, rate, strip, south, north, inc, coef, a, b, rates):
    fields = ctl.shape[0]
    tiles = coef.shape[1] // 8
    own_rates = (rate[0], rate[1])
    for k in range(2):
        for row, block in blocks(own_rates[k], south[fields + k], north[fields + k]):
            rates[2 * k, pl.ds(row, block.shape[0]), :] = block
        for row, block in blocks(strip[...], south[fields + 2], north[fields + 2]):
            lane = lanes(block.shape)
            near = (lane < HALO) | (lane >= block.shape[-1] - HALO)
            rates[2 * k + 1, pl.ds(row, block.shape[0]), :] = jnp.where(
                near, unpack(block, fields + k), 0.0
            )
        clear = jnp.zeros((PAD, rates.shape[2]), F32)
        for plane in (2 * k, 2 * k + 1):
            rates[plane, pl.ds(0, PAD), :] = clear
    for tile in range(tiles):
        here, down = pl.ds(PAD + 8 * tile, 8), pl.ds(PAD + 8 * tile - 1, 8)
        east = (rates[0, here, :], rates[1, here, :])
        west = turned(east[0], east[1], 1)
        for plane in range(2):
            n, s = rates[2 + plane, here, :], rates[2 + plane, down, :]
            e, w = east[plane], west[plane]
            for i, value in enumerate((1.0 - e - w - n - s, e, w, n, s)):
                coef[2 * i + plane, pl.ds(8 * tile, 8), :] = value
    load_field(a, ctl, strip, south, north)

    def finish(f, row, main):
        inc[f, pl.ds(row, 8), :] = main

    ten_steps(a, b, coef, finish, tiles)


def diffuse_pulled(pulled, strip, south, north, coef, ctl, grad, a, b):
    load_field(a, pulled, strip, south, north)

    def finish(f, row, main):
        grad[f, pl.ds(row, 8), :] = ctl[f, pl.ds(row, 8), :] + main

    ten_steps(a, b, coef, finish, coef.shape[1] // 8)


def tables(obs, holder, cell, out, slots):
    profiles = holder.shape[1]
    level_here = lax.axis_index("obs")
    groups = obs.shape[0] // 16
    width = obs.shape[1]
    acc = jnp.zeros((48, profiles), F32)
    row16 = subs((16, width))
    for z in range(groups):
        parts = ([], [], [])
        hots = []
        for c in range(4):
            at = 16 * z + c
            index = obs[pl.ds(at, 1), :].astype(I32)
            w, y, q = (obs[pl.ds(at + 4 * k, 1), :] for k in (1, 2, 3))
            prof = index & 511
            level = (index >> 9) & 7
            field = index >> 12
            low = jnp.where(level == level_here, q, 0.0)
            high = jnp.where(level == level_here - 1, q, 0.0)
            v = 1.0 - w
            lw, hv = low * w, high * v
            rows = (lw * w + hv * v, lw * v, hv * w, (lw + hv) * y)
            value = jnp.where(
                row16 < 8,
                jnp.where(row16 < 4, rows[0], rows[1]),
                jnp.where(row16 < 12, rows[2], rows[3]),
            )
            value = jnp.where((row16 & 3) == field, value, 0.0)
            for part, x in zip(parts, split3(value)):
                part.append(x)
            hots.append(one_hot(subs((profiles, width)) == prof))
        left = jnp.concatenate([jnp.concatenate(p, axis=1) for p in parts], axis=0)
        acc = acc + dot_nt(left, jnp.concatenate(hots, axis=1))
    table = acc[0:16] + acc[16:32] + acc[32:48]
    held = subs((out.shape[0], profiles)) == holder[...]
    held16 = one_hot(held)
    before = one_hot(subs((profiles, profiles)) < lanes((profiles, profiles)))
    slot = jnp.sum(jnp.where(held, dot_nn(held16, before), 0.0), axis=0, keepdims=True)
    slots[...] = slot
    place = slot.astype(I32)
    cells = cell[...].astype(F32)
    mine = [subs((8, profiles)) * 2 + k == place for k in range(2)]
    for k in range(2):
        value = jnp.concatenate(
            [jnp.where(mine[k], table[r : r + 1], 0.0) for r in range(16)], axis=0
        )
        total = sum(dot_nt(held16, part) for part in split3(value))
        out[:, k, :] = total
    value = jnp.concatenate(
        [jnp.where(mine[k], cells, 0.0) for k in range(2)]
        + [jnp.zeros((112, profiles), F32)],
        axis=0,
    )
    out[:, 2, :] = sum(dot_nt(held16, part) for part in split3(value)[:2])


def gather(inc, sent, found, tab, hold):
    fields = inc.shape[0]
    tab[pl.ds(0, 128), :] = jnp.concatenate([sent[:, 0, :], sent[:, 1, :]], axis=0).T
    cells = jnp.concatenate([sent[:, 2, :], sent[:, 2, :]], axis=0).T
    cells = jnp.where(lanes((8, 128)) < 64, cells[0:8], cells[8:16])
    tab[pl.ds(128, 8), :] = cells
    cells = cells.astype(I32)
    left = jnp.concatenate(
        [jnp.concatenate(split3(inc[f]), axis=1) for f in range(fields)], axis=0
    )
    for pair in range(4):
        hots, lats = [], []
        for s in (2 * pair, 2 * pair + 1):
            row = cells[s : s + 1]
            hots.append(one_hot(subs((128, 128)) == (row & 127)))
            lats.append(subs((128, 128)) == (row >> 7))
        hot = jnp.concatenate(hots, axis=1)
        hit = dot_nn(left, jnp.concatenate([hot, hot, hot], axis=0))
        for f in range(fields):
            for i in range(2):
                part = hit[128 * f : 128 * (f + 1), 128 * i : 128 * (i + 1)]
                hold[pl.ds(8 * f + 2 * pair + i, 1), :] = jnp.sum(
                    jnp.where(lats[i], part, 0.0), axis=0, keepdims=True
                )
    rows = hold[...]
    for z in range(found.shape[0] // rows.shape[0]):
        found[pl.ds(z * rows.shape[0], rows.shape[0]), :] = rows


def scatter(levels, tab, pulled, east, west, columns):
    fields = pulled.shape[0]
    rows = 8 * fields
    here = lax.axis_index("obs")
    top = levels.shape[0] // rows - 1

    def level(k):
        return levels[pl.ds(pl.multiple_of(jnp.clip(k, 0, top) * rows, rows), rows), :]

    own, above, below = level(here), level(here + 1), level(here - 1)
    d, o, u, b = (tab[pl.ds(rows * k, rows), :] for k in range(4))
    amount = d * own + o * above + u * below - b
    cells = tab[pl.ds(4 * rows, 8), :].astype(I32)
    lat = [subs((128, 128)) == (cells[s : s + 1] >> 7) for s in range(8)]
    hot = jnp.concatenate(
        [one_hot(subs((128, 128)) == (cells[s : s + 1] & 127)) for s in range(8)], axis=1
    )
    for f in range(fields):
        total = jnp.zeros((128, 128), F32)
        for part in split3(amount[8 * f : 8 * f + 8]):
            wide = part.astype(F32)
            left = jnp.concatenate(
                [jnp.where(lat[s], wide[s : s + 1], 0.0).astype(BF16) for s in range(8)], axis=1
            )
            total = total + dot_nt(left, hot)
        pulled[f] = total
    pack_edges([pulled[f] for f in range(fields)], east, west)
    for half in range(2):
        turned_block = levels[pl.ds(128 * half, 128), :].T
        for k in range(2):
            columns[:, 2 * k + half, :] = turned_block[64 * k : 64 * (k + 1)]


def depart(columns, holder, slots, prof, field, level, weight, innov, prec, out):
    profiles = holder.shape[1]
    left = jnp.concatenate(
        [
            jnp.concatenate([columns[:, half, :], columns[:, 2 + half, :]], axis=0).T
            for half in range(2)
        ],
        axis=0,
    )
    place = slots[...].astype(I32)
    row = subs((128, profiles))
    held = one_hot(((row & 63) == holder[...]) & ((row >> 6) == (place & 1)))
    spread = dot_nn(
        jnp.concatenate(split3(left), axis=1), jnp.concatenate([held, held, held], axis=0)
    )
    mine = subs((8, profiles)) == (place >> 1)
    values = jnp.concatenate(
        [
            jnp.sum(jnp.where(mine, spread[8 * r : 8 * r + 8], 0.0), axis=0, keepdims=True)
            for r in range(32)
        ],
        axis=0,
    )
    hot = jnp.concatenate(
        [one_hot(subs((profiles, 128)) == prof[pl.ds(c, 1), :]) for c in range(4)], axis=1
    )
    seen = sum(dot_nn(part, hot) for part in split3(values))
    row = subs((32, 128))
    for c in range(4):
        at = pl.ds(c, 1)
        code = level[at, :] * 4 + field[at, :]
        part = seen[:, 128 * c : 128 * (c + 1)]
        low = jnp.sum(jnp.where(row == code, part, 0.0), axis=0, keepdims=True)
        high = jnp.sum(jnp.where(row == code + 4, part, 0.0), axis=0, keepdims=True)
        w = weight[at, :]
        out[at, :] = prec[at, :] * (w * low + (1.0 - w) * high - innov[at, :])


def ring(axis, by):
    count = lax.axis_size(axis)
    return [(i, (i + by) % count) for i in range(count)]


def pair(forward, back, axis):
    return (
        lax.ppermute(forward, axis, ring(axis, 1)),
        lax.ppermute(back, axis, ring(axis, -1)),
    )


def exchange(x, axes):
    return lax.all_to_all(x, axes, 0, 0, tiled=True)


def assimilate(
    control,
    diffusivity,
    prof_tile,
    prof_cell,
    obs_prof,
    obs_field,
    obs_level,
    obs_weight,
    innovation,
    obs_precision,
):
    fields, _, ny, nx = control.shape
    tile = (ny, nx)
    profiles = prof_tile.shape[0]
    holders = lax.axis_size("gx") * lax.axis_size("gy")
    levels = lax.axis_size("obs")
    ext = ny + 2 * ROWS
    ctl = control.reshape(fields, ny, nx)
    rate = diffusivity.reshape(2, ny, nx)
    holder = prof_tile.reshape(1, profiles)
    cell = prof_cell.reshape(1, profiles)
    obs = [
        x.reshape(4, 128)
        for x in (obs_prof, obs_field, obs_level, obs_weight, innovation, obs_precision)
    ]
    planes = pltpu.VMEM((2 * fields, ext + 2 * PAD, nx), F32)

    given = [pltpu.with_memory_space_constraint(x, pltpu.HBM) for x in (ctl, rate, holder, cell, *obs)]
    east, west, rows, ctl, rate, holder, cell, *obs = call(
        pack_inputs,
        [tile, tile, (levels * 16, 128)] + [jax.ShapeDtypeStruct(x.shape, x.dtype) for x in given],
        given,
        [pltpu.SemaphoreType.DMA((len(given),))],
        hbm=True,
    )
    left, right = pair(east, west, "gx")
    rows = exchange(rows, "obs")
    side = (fields + 3, ROWS, nx)
    strip, north, south = call(edges_first, [tile, side, side], [ctl, rate, left, right])
    south, north = pair(north, south, "gy")
    table, slots = call(
        tables, [(holders, 3, 128), (1, profiles)], [rows, holder, cell], flops=400_000_000
    )
    table = exchange(table, ("gx", "gy"))
    inc, coef = call(
        diffuse_control,
        [(fields, ny, nx), (10, ext, nx)],
        [ctl, rate, strip, south, north],
        [planes, planes, pltpu.VMEM((4, ext + 2 * PAD, nx), F32)],
        flops=40_000_000,
    )
    found, tab = call(
        gather,
        [(levels * fields * 8, 128), (136, 128)],
        [inc, table],
        [pltpu.VMEM((fields * 8, 128), F32)],
        flops=400_000_000,
    )
    found = exchange(found, "obs")
    pulled, east, west, columns = call(
        scatter,
        [(fields, ny, nx), tile, tile, (holders, 4, 128)],
        [found, tab],
        flops=400_000_000,
    )
    left, right = pair(east, west, "gx")
    columns = exchange(columns, ("gx", "gy"))
    side = (fields + 1, ROWS, nx)
    strip, north, south = call(edges_second, [tile, side, side], [pulled, left, right])
    south, north = pair(north, south, "gy")
    (gradient,) = call(
        diffuse_pulled,
        [(fields, ny, nx)],
        [pulled, strip, south, north, coef, ctl],
        [planes, planes],
        flops=40_000_000,
    )
    (departures,) = call(depart, [(4, 128)], [columns, holder, slots, *obs], flops=400_000_000)
    return gradient.reshape(control.shape), departures.reshape(obs_prof.shape)


def solution(mesh):
    in_specs = (
        P(None, "obs", "gy", "gx"),
        P(None, "obs", "gy", "gx"),
        P(("gx", "gy"), None),
        P(("gx", "gy")),
        P(("gx", "gy", "obs")),
        P(("gx", "gy", "obs")),
        P(("gx", "gy", "obs")),
        P(("gx", "gy", "obs")),
        P(("gx", "gy", "obs")),
        P(("gx", "gy", "obs")),
    )
    out_specs = (P(None, "obs", "gy", "gx"), P(("gx", "gy", "obs")))
    return jax.shard_map(
        assimilate, mesh=mesh, in_specs=in_specs, out_specs=out_specs, check_vma=False
    )
```

profile of v0, /device:TPU:24, one launch (start us, length us, event | category | flops | bytes accessed | tf_op | source)
XLA Modules:
  0.0 99.2 jit_solution(1683404918336887694)
XLA Ops:
  0.6 1.4 %shard_map.113 = (f32[128,128]{1,0:T(8,128)S(1)}, f32[128,128]{1,0:T(8,128)S(1)}, f32[128,128]{1,0:T(8,128)S(1)}, f32[4,128,128]{2,1,0:T(8,128)S(1)}, f32[2,128,...) custom-call(f32[4,128,128]{2,1,0:T(8,128)} %bitcast.22, ...), custom_call_target="tpu_custom_call" | custom-call | flops 1000000 | bytes 1015808 | tf_op jit(solution)/shard_map/pallas_call | solution.py:49
  2.0 18.5 %all_to_all.32 = f32[8,16,128]{2,1,0:T(8,128)S(1)} all-to-all(f32[8,16,128]{2,1,0:T(8,128)S(1)} %bitcast.20), channel_id=1, replica_groups=mesh['gx'=8,'gy'=8,'obs'=8] {'obs'}, dimensions={0} | all-to-all | bytes 131072 | tf_op jit(solution)/shard_map/all_to_all | solution.py:410
  20.5 2.6 %shard_map.116 = (f32[64,3,128]{2,1,0:T(4,128)}, f32[1,512]{1,0:T(1,128)S(1)}) custom-call(f32[128,128]{1,0:T(8,128)S(1)} %bitcast.21, s32[1,512]{1,0:T(1,128)S(1)} %get-tuple-element.40.holder, s32[1,512]{1,0:T(1,128)S(1)} %get-tuple-element.41.cell), custom_call_target="tpu_custom_call" | custom-call | flops 400000000 | bytes 169984 | tf_op jit(solution)/shard_map/pallas_call | solution.py:49
  23.1 10.3 %all-to-all-start.1 = ((f32[64,3,128]{2,1,0:T(4,128)}), f32[64,3,128]{2,1,0:T(4,128)S(1)}, u32[]{:S(2)}, u32[]{:S(2)}) async-start(f32[64,3,128]{2,1,0:T(4,128)} %get-tuple-element.42), calls=%async_computation.1 | async-start | bytes 262144 | tf_op jit(solution)/shard_map/all_to_all | solution.py:410
  33.4 0.1 collective-permute-start
  33.6 2.8 %collective-permute-start.1 = (f32[128,128]{1,0:T(8,128)S(1)}, f32[128,128]{1,0:T(8,128)S(1)}, u32[]{:S(2)}, u32[]{:S(2)}) collective-permute-start(f32[128,128]{1,0:T(8,128)S(1)} %get-tuple-element.34), channel_id=1, source_target_pairs={{0,448},{64,0},{128,64},{192,128},{256,192},{320,256},{384,320},{4... | collective-permute-start | bytes 196616 | tf_op jit(solution)/shard_map/ppermute | solution.py:405
  36.4 2.3 %collective-permute-done.left = f32[128,128]{1,0:T(8,128)S(1)} collective-permute-done((f32[128,128]{1,0:T(8,128)S(1)}, f32[128,128]{1,0:T(8,128)S(1)}, u32[]{:S(2)}, u32[]{:S(2)}) %collective-permute-start) | collective-permute-done | bytes 65568 | tf_op jit(solution)/shard_map/ppermute | solution.py:404
  38.6 0.0 collective-permute-done.1.right
  38.7 4.9 %collective-permute-start.2 = (f32[7,16,128]{2,1,0:T(8,128)S(1)}, f32[7,16,128]{2,1,0:T(8,128)S(1)}, u32[]{:S(2)}, u32[]{:S(2)}) collective-permute-start(f32[7,16,128]{2,1,0:T(8,128)S(1)} %get-tuple-element.36), channel_id=1, source_target_pairs={{0,8},{8,16},{16,24},{24,32},{32,40},{40,48},{48,56},{56,0},{1,9},... | collective-permute-start | bytes 172040 | tf_op jit(solution)/shard_map/ppermute | solution.py:404
  43.6 1.9 %collective-permute-start.3 = (f32[7,16,128]{2,1,0:T(8,128)S(1)}, f32[7,16,128]{2,1,0:T(8,128)S(1)}, u32[]{:S(2)}, u32[]{:S(2)}) collective-permute-start(f32[7,16,128]{2,1,0:T(8,128)S(1)} %get-tuple-element.37), channel_id=1, source_target_pairs={{0,56},{8,0},{16,8},{24,16},{32,24},{40,32},{48,40},{56,48},{1,57}... | collective-permute-start | bytes 172040 | tf_op jit(solution)/shard_map/ppermute | solution.py:405
  45.5 0.0 collective-permute-done.2.south
  45.5 5.3 %collective-permute-done.3.north = f32[7,16,128]{2,1,0:T(8,128)S(1)} collective-permute-done((f32[7,16,128]{2,1,0:T(8,128)S(1)}, f32[7,16,128]{2,1,0:T(8,128)S(1)}, u32[]{:S(2)}, u32[]{:S(2)}) %collective-permute-start.3) | collective-permute-done | bytes 57376 | tf_op jit(solution)/shard_map/ppermute | solution.py:405
  50.9 3.7 %shard_map.115 = (f32[4,128,128]{2,1,0:T(8,128)S(1)}, f32[10,160,128]{2,1,0:T(8,128)S(1)}) custom-call(f32[4,128,128]{2,1,0:T(8,128)S(1)} %get-tuple-element.31.ctl, f32[2,128,128]{2,1,0:T(8,128)S(1)} %get-tuple-element.32.rate, f32[128,128]{1,0:T(8,128)S(1)} %get-tuple-element.35.strip, f32[7,16,128]{2,1,0:T(8,128)S(1)} %collective-permute-done.2.south, ...), custom_call_target="tpu_custom_call" | custom-call | flops 40000000 | bytes 1654784 | tf_op jit(solution)/shard_map/pallas_call | solution.py:49
  54.5 0.0 all-to-all-done.1.sent
  54.6 0.9 shard_map.117
  55.4 11.5 %all_to_all.33 = f32[8,32,128]{2,1,0:T(8,128)S(1)} all-to-all(f32[8,32,128]{2,1,0:T(8,128)S(1)} %bitcast.19), channel_id=1, replica_groups=mesh['gx'=8,'gy'=8,'obs'=8] {'obs'}, dimensions={0} | all-to-all | bytes 262144 | tf_op jit(solution)/shard_map/all_to_all | solution.py:410
  66.9 1.9 %shard_map.118 = (f32[4,128,128]{2,1,0:T(8,128)S(1)}, f32[128,128]{1,0:T(8,128)S(1)}, f32[128,128]{1,0:T(8,128)S(1)}, f32[64,4,128]{2,1,0:T(4,128)}) custom-call(f32[256,128]{1,0:T(8,128)S(1)} %bitcast.18, f32[136,128]{1,0:T(8,128)S(1)} %get-tuple-element.44.tab), custom_call_target="tpu_custom_call" | custom-call | flops 400000000 | bytes 724992 | tf_op jit(solution)/shard_map/pallas_call | solution.py:49
  68.7 7.6 %all-to-all-start.3 = ((f32[64,4,128]{2,1,0:T(4,128)}), f32[64,4,128]{2,1,0:T(4,128)S(1)}, u32[]{:S(2)}, u32[]{:S(2)}) async-start(f32[64,4,128]{2,1,0:T(4,128)} %get-tuple-element.52), calls=%async_computation.3 | async-start | bytes 262144 | tf_op jit(solution)/shard_map/all_to_all | solution.py:410
  76.3 0.1 collective-permute-start.4
  76.4 2.8 %collective-permute-start.5 = (f32[128,128]{1,0:T(8,128)S(1)}, f32[128,128]{1,0:T(8,128)S(1)}, u32[]{:S(2)}, u32[]{:S(2)}) collective-permute-start(f32[128,128]{1,0:T(8,128)S(1)} %get-tuple-element.47), channel_id=1, source_target_pairs={{0,448},{64,0},{128,64},{192,128},{256,192},{320,256},{384,320},{4... | collective-permute-start | bytes 196616 | tf_op jit(solution)/shard_map/ppermute | solution.py:405
  79.3 2.3 %collective-permute-done.4.left = f32[128,128]{1,0:T(8,128)S(1)} collective-permute-done((f32[128,128]{1,0:T(8,128)S(1)}, f32[128,128]{1,0:T(8,128)S(1)}, u32[]{:S(2)}, u32[]{:S(2)}) %collective-permute-start.4) | collective-permute-done | bytes 65568 | tf_op jit(solution)/shard_map/ppermute | solution.py:404
  81.5 0.0 collective-permute-done.5.right
  81.5 4.9 %collective-permute-start.6 = (f32[5,16,128]{2,1,0:T(8,128)S(1)}, f32[5,16,128]{2,1,0:T(8,128)S(1)}, u32[]{:S(2)}, u32[]{:S(2)}) collective-permute-start(f32[5,16,128]{2,1,0:T(8,128)S(1)} %get-tuple-element.49), channel_id=1, source_target_pairs={{0,8},{8,16},{16,24},{24,32},{32,40},{40,48},{48,56},{56,0},{1,9},... | collective-permute-start | bytes 122888 | tf_op jit(solution)/shard_map/ppermute | solution.py:404
  86.5 1.9 %collective-permute-start.7 = (f32[5,16,128]{2,1,0:T(8,128)S(1)}, f32[5,16,128]{2,1,0:T(8,128)S(1)}, u32[]{:S(2)}, u32[]{:S(2)}) collective-permute-start(f32[5,16,128]{2,1,0:T(8,128)S(1)} %get-tuple-element.50), channel_id=1, source_target_pairs={{0,56},{8,0},{16,8},{24,16},{32,24},{40,32},{48,40},{56,48},{1,57}... | collective-permute-start | bytes 122888 | tf_op jit(solution)/shard_map/ppermute | solution.py:405
  88.4 0.0 collective-permute-done.6.south
  88.4 5.2 %collective-permute-done.7.north = f32[5,16,128]{2,1,0:T(8,128)S(1)} collective-permute-done((f32[5,16,128]{2,1,0:T(8,128)S(1)}, f32[5,16,128]{2,1,0:T(8,128)S(1)}, u32[]{:S(2)}, u32[]{:S(2)}) %collective-permute-start.7) | collective-permute-done | bytes 40992 | tf_op jit(solution)/shard_map/ppermute | solution.py:405
  93.6 4.2 %shard_map.120 = f32[4,128,128]{2,1,0:T(8,128)} custom-call(f32[4,128,128]{2,1,0:T(8,128)S(1)} %get-tuple-element.45.pulled, f32[128,128]{1,0:T(8,128)S(1)} %get-tuple-element.48.strip, f32[5,16,128]{2,1,0:T(8,128)S(1)} %collective-permute-done.6.south, f32[5,16,128]{2,1,0:T(8,128)S(1)} %collective-permute-done.7.north, ...), custom_call_target="tpu_custom_call" | custom-call | flops 40000000 | bytes 1753088 | tf_op jit(solution)/shard_map/pallas_call | solution.py:49
  97.8 0.0 all-to-all-done.3.columns
  97.8 1.4 %shard_map.121 = f32[4,128]{1,0:T(4,128)} custom-call(f32[64,4,128]{2,1,0:T(4,128)S(1)} %all-to-all-done.3.columns, s32[1,512]{1,0:T(1,128)S(1)} %get-tuple-element.40.holder, f32[1,512]{1,0:T(1,128)S(1)} %get-tuple-element.53.slots, s32[4,128]{1,0:T(4,128)S(1)} %get-tuple-element.54.prof, s32[4,128]{1,0:T(4,128)S(1)} %get-tuple-element.55.field, ...), custom_call_target="tpu_custom_call" | custom-call | flops 400000000 | bytes 149504 | tf_op jit(solution)/shard_map/pallas_call | solution.py:49
  (2 shorter events, 0.0 us)
Async XLA Ops:
  23.1 31.5 %all-to-all-start.1 = ((f32[64,3,128]{2,1,0:T(4,128)}), f32[64,3,128]{2,1,0:T(4,128)S(1)}, u32[]{:S(2)}, u32[]{:S(2)}) async-start(f32[64,3,128]{2,1,0:T(4,128)} %get-tuple-element.42), calls=%async_computation.1 | async-start | bytes 262144 | tf_op jit(solution)/shard_map/all_to_all | solution.py:410
  33.4 5.2 %collective-permute-start = (f32[128,128]{1,0:T(8,128)S(1)}, f32[128,128]{1,0:T(8,128)S(1)}, u32[]{:S(2)}, u32[]{:S(2)}) collective-permute-start(f32[128,128]{1,0:T(8,128)S(1)} %get-tuple-element.33), channel_id=1, source_target_pairs={{0,64},{64,128},{128,192},{192,256},{256,320},{320,384},{384,448},... | collective-permute-start | bytes 196616 | tf_op jit(solution)/shard_map/ppermute | solution.py:404
  33.6 5.1 %collective-permute-start.1 = (f32[128,128]{1,0:T(8,128)S(1)}, f32[128,128]{1,0:T(8,128)S(1)}, u32[]{:S(2)}, u32[]{:S(2)}) collective-permute-start(f32[128,128]{1,0:T(8,128)S(1)} %get-tuple-element.34), channel_id=1, source_target_pairs={{0,448},{64,0},{128,64},{192,128},{256,192},{320,256},{384,320},{4... | collective-permute-start | bytes 196616 | tf_op jit(solution)/shard_map/ppermute | solution.py:405
  38.7 6.8 %collective-permute-start.2 = (f32[7,16,128]{2,1,0:T(8,128)S(1)}, f32[7,16,128]{2,1,0:T(8,128)S(1)}, u32[]{:S(2)}, u32[]{:S(2)}) collective-permute-start(f32[7,16,128]{2,1,0:T(8,128)S(1)} %get-tuple-element.36), channel_id=1, source_target_pairs={{0,8},{8,16},{16,24},{24,32},{32,40},{40,48},{48,56},{56,0},{1,9},... | collective-permute-start | bytes 172040 | tf_op jit(solution)/shard_map/ppermute | solution.py:404
  43.6 7.3 %collective-permute-start.3 = (f32[7,16,128]{2,1,0:T(8,128)S(1)}, f32[7,16,128]{2,1,0:T(8,128)S(1)}, u32[]{:S(2)}, u32[]{:S(2)}) collective-permute-start(f32[7,16,128]{2,1,0:T(8,128)S(1)} %get-tuple-element.37), channel_id=1, source_target_pairs={{0,56},{8,0},{16,8},{24,16},{32,24},{40,32},{48,40},{56,48},{1,57}... | collective-permute-start | bytes 172040 | tf_op jit(solution)/shard_map/ppermute | solution.py:405
  68.7 29.1 %all-to-all-start.3 = ((f32[64,4,128]{2,1,0:T(4,128)}), f32[64,4,128]{2,1,0:T(4,128)S(1)}, u32[]{:S(2)}, u32[]{:S(2)}) async-start(f32[64,4,128]{2,1,0:T(4,128)} %get-tuple-element.52), calls=%async_computation.3 | async-start | bytes 262144 | tf_op jit(solution)/shard_map/all_to_all | solution.py:410
  76.3 5.2 %collective-permute-start.4 = (f32[128,128]{1,0:T(8,128)S(1)}, f32[128,128]{1,0:T(8,128)S(1)}, u32[]{:S(2)}, u32[]{:S(2)}) collective-permute-start(f32[128,128]{1,0:T(8,128)S(1)} %get-tuple-element.46), channel_id=1, source_target_pairs={{0,64},{64,128},{128,192},{192,256},{256,320},{320,384},{384,448},... | collective-permute-start | bytes 196616 | tf_op jit(solution)/shard_map/ppermute | solution.py:404
  76.4 5.1 %collective-permute-start.5 = (f32[128,128]{1,0:T(8,128)S(1)}, f32[128,128]{1,0:T(8,128)S(1)}, u32[]{:S(2)}, u32[]{:S(2)}) collective-permute-start(f32[128,128]{1,0:T(8,128)S(1)} %get-tuple-element.47), channel_id=1, source_target_pairs={{0,448},{64,0},{128,64},{192,128},{256,192},{320,256},{384,320},{4... | collective-permute-start | bytes 196616 | tf_op jit(solution)/shard_map/ppermute | solution.py:405
  81.5 6.8 %collective-permute-start.6 = (f32[5,16,128]{2,1,0:T(8,128)S(1)}, f32[5,16,128]{2,1,0:T(8,128)S(1)}, u32[]{:S(2)}, u32[]{:S(2)}) collective-permute-start(f32[5,16,128]{2,1,0:T(8,128)S(1)} %get-tuple-element.49), channel_id=1, source_target_pairs={{0,8},{8,16},{16,24},{24,32},{32,40},{40,48},{48,56},{56,0},{1,9},... | collective-permute-start | bytes 122888 | tf_op jit(solution)/shard_map/ppermute | solution.py:404
  86.5 7.1 %collective-permute-start.7 = (f32[5,16,128]{2,1,0:T(8,128)S(1)}, f32[5,16,128]{2,1,0:T(8,128)S(1)}, u32[]{:S(2)}, u32[]{:S(2)}) collective-permute-start(f32[5,16,128]{2,1,0:T(8,128)S(1)} %get-tuple-element.50), channel_id=1, source_target_pairs={{0,56},{8,0},{16,8},{24,16},{32,24},{40,32},{48,40},{56,48},{1,57}... | collective-permute-start | bytes 122888 | tf_op jit(solution)/shard_map/ppermute | solution.py:405
where the time goes:
time: 99.7 us; the launch traced here: 99.2 us
  starting transfers between devices  37.5 us (38%)
  blocking collectives  30 us (30%)
  Pallas kernels  16 us (16%)
  waiting for transfers between devices  15 us (15%)
    all_to_all x2, blocking collectives, exchange(): return lax.all_to_all(x, axes, 0, 0, tiled=True)  30 us
    all_to_all x2, starting transfers between devices, exchange(): return lax.all_to_all(x, axes, 0, 0, tiled=True)  17.9 us
    pallas_call x9, Pallas kernels, call(): pl.pallas_call(body, out_shape=outs, in_specs=[given] * len(args), out_sp...  16 us
    ppermute x4, waiting for transfers between devices, pair(): lax.ppermute(back, axis, ring(axis, -1))  10.5 us
    ppermute x4, starting transfers between devices, pair(): lax.ppermute(forward, axis, ring(axis, 1))  10.1 us
    ppermute x4, starting transfers between devices, pair(): lax.ppermute(back, axis, ring(axis, -1))  9.51 us
    ppermute x4, waiting for transfers between devices, pair(): lax.ppermute(forward, axis, ring(axis, 1))  4.51 us
  transfers between devices with their start and end apart: 10, of which 4 were waited for; matrix products, arithmetic and copies ran while one was open for 0% of the time, Pallas kernels for 8%

commit v1 on v0

--- a/solution.py
+++ b/solution.py
@@ -103,23 +103,30 @@
         obs[pl.ds(z * rows.shape[0], rows.shape[0]), :] = rows
 
 
-def north_south(arrays, strip, north_ref, south_ref):
-    for a, x in enumerate(arrays + [strip]):
-        north_ref[a] = x[x.shape[0] - ROWS :]
-        south_ref[a] = x[:ROWS]
-
-
-def edges_first(ctl, rate, left, right, strip, north, south):
-    joined = left[...] + right[...]
-    strip[...] = joined
-    arrays = [ctl[f] for f in range(ctl.shape[0])] + [rate[0], rate[1]]
-    north_south(arrays, joined, north, south)
-
-
-def edges_second(pulled, left, right, strip, north, south):
-    joined = left[...] + right[...]
-    strip[...] = joined
-    north_south([pulled[f] for f in range(pulled.shape[0])], joined, north, south)
+def odd():
+    return lax.rem(lax.axis_index("gy"), 2)
+
+
+def pick(first, second):
+    return pl.multiple_of(jnp.where(odd() == 0, first, second), 8)
+
+
+def meet(refs, strip, first, second):
+    last = strip.shape[0] - ROWS
+    for target, at in ((first, pick(last, 0)), (second, pick(0, last))):
+        for a, ref in enumerate(refs + [strip]):
+            target[a] = ref[pl.ds(at, ROWS), :]
+
+
+def edges_first(ctl, rate, left, right, strip, first, second):
+    strip[...] = left[...] + right[...]
+    refs = [ctl.at[f] for f in range(ctl.shape[0])] + [rate.at[0], rate.at[1]]
+    meet(refs, strip, first, second)
+
+
+def edges_second(pulled, left, right, strip, first, second):
+    strip[...] = left[...] + right[...]
+    meet([pulled.at[f] for f in range(pulled.shape[0])], strip, first, second)
 
 
 def unpack(block, a):
@@ -129,9 +136,9 @@
     return jnp.where(lanes(block.shape) < width // 2, east, west)
 
 
-def blocks(own, south, north):
-    height = own.shape[0]
-    return ((PAD, south), (PAD + ROWS, own), (PAD + ROWS + height, north))
+def blocks(own, first, second):
+    low, high = PAD, PAD + ROWS + own.shape[0]
+    return ((pick(high, low), first), (PAD + ROWS, own), (pick(low, high), second))
 
 
 def turned(main, beyond, by):
@@ -182,12 +189,12 @@
     one_step(b, coef, store, ROWS // 8, tiles - ROWS // 8)
 
 
-def load_field(a, own, strip, south, north):
+def load_field(a, own, strip, first, second, packed):
     fields = own.shape[0]
     for f in range(fields):
-        for row, block in blocks(own[f], south[f], north[f]):
+        for row, block in blocks(own[f], first[f], second[f]):
             a[2 * f, pl.ds(row, block.shape[0]), :] = block
-    for row, block in blocks(strip[...], south[south.shape[0] - 1], north[north.shape[0] - 1]):
+    for row, block in blocks(strip[...], first[packed], second[packed]):
         for f in range(fields):
             a[2 * f + 1, pl.ds(row, block.shape[0]), :] = unpack(block, f)
     clear = jnp.zeros((PAD, a.shape[2]), F32)
@@ -196,14 +203,14 @@
         a[plane, pl.ds(a.shape[1] - PAD, PAD), :] = clear
 
 
-def diffuse_control(ctl, rate, strip, south, north, inc, coef, a, b, rates):
+def diffuse_control(ctl, rate, strip, first, second, inc, coef, a, b, rates):
     fields = ctl.shape[0]
     tiles = coef.shape[1] // 8
     own_rates = (rate[0], rate[1])
     for k in range(2):
-        for row, block in blocks(own_rates[k], south[fields + k], north[fields + k]):
+        for row, block in blocks(own_rates[k], first[fields + k], second[fields + k]):
             rates[2 * k, pl.ds(row, block.shape[0]), :] = block
-        for row, block in blocks(strip[...], south[fields + 2], north[fields + 2]):
+        for row, block in blocks(strip[...], first[fields + 2], second[fields + 2]):
             lane = lanes(block.shape)
             near = (lane < HALO) | (lane >= block.shape[-1] - HALO)
             rates[2 * k + 1, pl.ds(row, block.shape[0]), :] = jnp.where(
@@ -221,7 +228,7 @@
             e, w = east[plane], west[plane]
             for i, value in enumerate((1.0 - e - w - n - s, e, w, n, s)):
                 coef[2 * i + plane, pl.ds(8 * tile, 8), :] = value
-    load_field(a, ctl, strip, south, north)
+    load_field(a, ctl, strip, first, second, fields + 2)
 
     def finish(f, row, main):
         inc[f, pl.ds(row, 8), :] = main
@@ -229,8 +236,8 @@
     ten_steps(a, b, coef, finish, tiles)
 
 
-def diffuse_pulled(pulled, strip, south, north, coef, ctl, grad, a, b):
-    load_field(a, pulled, strip, south, north)
+def diffuse_pulled(pulled, strip, first, second, coef, ctl, grad, a, b):
+    load_field(a, pulled, strip, first, second, pulled.shape[0])
 
     def finish(f, row, main):
         grad[f, pl.ds(row, 8), :] = ctl[f, pl.ds(row, 8), :] + main
@@ -285,19 +292,20 @@
             [jnp.where(mine[k], table[r : r + 1], 0.0) for r in range(16)], axis=0
         )
         total = sum(dot_nt(held16, part) for part in split3(value))
-        out[:, k, :] = total
+        out[:, 0, pl.ds(128 * k, 128)] = total
     value = jnp.concatenate(
         [jnp.where(mine[k], cells, 0.0) for k in range(2)]
         + [jnp.zeros((112, profiles), F32)],
         axis=0,
     )
-    out[:, 2, :] = sum(dot_nt(held16, part) for part in split3(value)[:2])
+    out[:, 0, pl.ds(256, 128)] = sum(dot_nt(held16, part) for part in split3(value)[:2])
 
 
 def gather(inc, sent, found, tab, hold):
     fields = inc.shape[0]
-    tab[pl.ds(0, 128), :] = jnp.concatenate([sent[:, 0, :], sent[:, 1, :]], axis=0).T
-    cells = jnp.concatenate([sent[:, 2, :], sent[:, 2, :]], axis=0).T
+    tab[pl.ds(0, 128), :] = jnp.concatenate([sent[:, 0, pl.ds(0, 128)], sent[:, 0, pl.ds(128, 128)]], axis=0).T
+    cells = sent[:, 0, pl.ds(256, 128)]
+    cells = jnp.concatenate([cells, cells], axis=0).T
     cells = jnp.where(lanes((8, 128)) < 64, cells[0:8], cells[8:16])
     tab[pl.ds(128, 8), :] = cells
     cells = cells.astype(I32)
@@ -404,6 +412,13 @@
         lax.ppermute(forward, axis, ring(axis, 1)),
         lax.ppermute(back, axis, ring(axis, -1)),
     )
+
+
+def swap(first, second, axis):
+    count = lax.axis_size(axis)
+    low = [(i, i ^ 1) for i in range(count)]
+    high = [(i, (i + 1 ^ 1) - 1) for i in range(1, count - 1)]
+    return lax.ppermute(first, axis, low), lax.ppermute(second, axis, high)
 
 
 def exchange(x, axes):
@@ -449,16 +464,16 @@
     left, right = pair(east, west, "gx")
     rows = exchange(rows, "obs")
     side = (fields + 3, ROWS, nx)
-    strip, north, south = call(edges_first, [tile, side, side], [ctl, rate, left, right])
-    south, north = pair(north, south, "gy")
+    strip, first, second = call(edges_first, [tile, side, side], [ctl, rate, left, right])
+    first, second = swap(first, second, "gy")
     table, slots = call(
-        tables, [(holders, 3, 128), (1, profiles)], [rows, holder, cell], flops=400_000_000
+        tables, [(holders, 1, 384), (1, profiles)], [rows, holder, cell], flops=400_000_000
     )
     table = exchange(table, ("gx", "gy"))
     inc, coef = call(
         diffuse_control,
         [(fields, ny, nx), (10, ext, nx)],
-        [ctl, rate, strip, south, north],
+        [ctl, rate, strip, first, second],
         [planes, planes, pltpu.VMEM((4, ext + 2 * PAD, nx), F32)],
         flops=40_000_000,
     )
@@ -479,12 +494,12 @@
     left, right = pair(east, west, "gx")
     columns = exchange(columns, ("gx", "gy"))
     side = (fields + 1, ROWS, nx)
-    strip, north, south = call(edges_second, [tile, side, side], [pulled, left, right])
-    south, north = pair(north, south, "gy")
+    strip, first, second = call(edges_second, [tile, side, side], [pulled, left, right])
+    first, second = swap(first, second, "gy")
     (gradient,) = call(
         diffuse_pulled,
         [(fields, ny, nx)],
-        [pulled, strip, south, north, coef, ctl],
+        [pulled, strip, first, second, coef, ctl],
         [planes, planes],
         flops=40_000_000,
     )

time: 99.7 us -> 97.6 us (0.979)
  the two profiles are of different devices: /device:TPU:24 before, /device:TPU:32 now
where the time goes in v1:
time: 97.6 us; the launch traced here: 97.2 us
  starting transfers between devices  35.2 us (36%)
  blocking collectives  30 us (31%)
  Pallas kernels  16.2 us (17%)
  waiting for transfers between devices  15.1 us (15%)
    all_to_all x2, blocking collectives, exchange(): return lax.all_to_all(x, axes, 0, 0, tiled=True)  30 us
    all_to_all x2, starting transfers between devices, exchange(): return lax.all_to_all(x, axes, 0, 0, tiled=True)  20.1 us
    pallas_call x9, Pallas kernels, call(): pl.pallas_call(body, out_shape=outs, in_specs=[given] * len(args), out_sp...  16.2 us
    ppermute x4, waiting for transfers between devices, swap(): return (lax.ppermute(first, axis, low), lax.ppermute(second, axis, high))  9.86 us
    ppermute x4, starting transfers between devices, swap(): return (lax.ppermute(first, axis, low), lax.ppermute(second, axis, high))  9.12 us
    ppermute x2, starting transfers between devices, pair(): lax.ppermute(back, axis, ring(axis, -1))  5.67 us
    ppermute x2, waiting for transfers between devices, pair(): lax.ppermute(forward, axis, ring(axis, 1))  5.27 us
  transfers between devices with their start and end apart: 10, of which 6 were waited for; matrix products, arithmetic and copies ran while one was open for 0% of the time, Pallas kernels for 8%

profile of v1, /device:TPU:32, one launch (start us, length us, event | category | flops | bytes accessed | tf_op | source)
XLA Modules:
  0.0 97.2 jit_solution(2452316448453954576)
XLA Ops:
  0.6 1.4 %shard_map.113 = (f32[128,128]{1,0:T(8,128)S(1)}, f32[128,128]{1,0:T(8,128)S(1)}, f32[128,128]{1,0:T(8,128)S(1)}, f32[4,128,128]{2,1,0:T(8,128)S(1)}, f32[2,128,...) custom-call(f32[4,128,128]{2,1,0:T(8,128)} %bitcast.22, ...), custom_call_target="tpu_custom_call" | custom-call | flops 1000000 | bytes 1015808 | tf_op jit(solution)/shard_map/pallas_call | solution.py:49
  2.0 18.5 %all_to_all.32 = f32[8,16,128]{2,1,0:T(8,128)S(1)} all-to-all(f32[8,16,128]{2,1,0:T(8,128)S(1)} %bitcast.20), channel_id=1, replica_groups=mesh['gx'=8,'gy'=8,'obs'=8] {'obs'}, dimensions={0} | all-to-all | bytes 131072 | tf_op jit(solution)/shard_map/all_to_all | solution.py:425
  20.5 2.6 %shard_map.116 = (f32[64,1,384]{2,1,0:T(1,128)}, f32[1,512]{1,0:T(1,128)S(1)}) custom-call(f32[128,128]{1,0:T(8,128)S(1)} %bitcast.21, s32[1,512]{1,0:T(1,128)S(1)} %get-tuple-element.40.holder, s32[1,512]{1,0:T(1,128)S(1)} %get-tuple-element.41.cell), custom_call_target="tpu_custom_call" | custom-call | flops 400000000 | bytes 169984 | tf_op jit(solution)/shard_map/pallas_call | solution.py:49
  23.1 10.2 %all-to-all-start.1 = ((f32[64,1,384]{2,1,0:T(1,128)}), f32[64,1,384]{2,1,0:T(1,128)S(1)}, u32[]{:S(2)}, u32[]{:S(2)}) async-start(f32[64,1,384]{2,1,0:T(1,128)} %get-tuple-element.42), calls=%async_computation.1 | async-start | bytes 196608 | tf_op jit(solution)/shard_map/all_to_all | solution.py:425
  33.3 0.1 collective-permute-start
  33.4 2.8 %collective-permute-start.1 = (f32[128,128]{1,0:T(8,128)S(1)}, f32[128,128]{1,0:T(8,128)S(1)}, u32[]{:S(2)}, u32[]{:S(2)}) collective-permute-start(f32[128,128]{1,0:T(8,128)S(1)} %get-tuple-element.34), channel_id=1, source_target_pairs={{0,448},{64,0},{128,64},{192,128},{256,192},{320,256},{384,320},{4... | collective-permute-start | bytes 196616 | tf_op jit(solution)/shard_map/ppermute | solution.py:413
  36.3 2.7 %collective-permute-done.left = f32[128,128]{1,0:T(8,128)S(1)} collective-permute-done((f32[128,128]{1,0:T(8,128)S(1)}, f32[128,128]{1,0:T(8,128)S(1)}, u32[]{:S(2)}, u32[]{:S(2)}) %collective-permute-start) | collective-permute-done | bytes 65568 | tf_op jit(solution)/shard_map/ppermute | solution.py:412
  39.0 0.0 collective-permute-done.1.right
  39.0 2.2 %collective-permute-start.2 = (f32[7,16,128]{2,1,0:T(8,128)S(1)}, f32[7,16,128]{2,1,0:T(8,128)S(1)}, u32[]{:S(2)}, u32[]{:S(2)}) collective-permute-start(f32[7,16,128]{2,1,0:T(8,128)S(1)} %get-tuple-element.36), channel_id=1, source_target_pairs={{0,8},{8,0},{16,24},{24,16},{32,40},{40,32},{48,56},{56,48},{1,9},... | collective-permute-start | bytes 172040 | tf_op jit(solution)/shard_map/ppermute | solution.py:421
  41.2 2.3 %collective-permute-start.3 = (f32[7,16,128]{2,1,0:T(8,128)S(1)}, f32[7,16,128]{2,1,0:T(8,128)S(1)}, u32[]{:S(2)}, u32[]{:S(2)}) collective-permute-start(f32[7,16,128]{2,1,0:T(8,128)S(1)} %get-tuple-element.37), channel_id=1, source_target_pairs={{8,16},{16,8},{24,32},{32,24},{40,48},{48,40},{9,17},{17,9},{25,33... | collective-permute-start | bytes 172040 | tf_op jit(solution)/shard_map/ppermute | solution.py:421
  43.5 1.6 %collective-permute-done.2.first = f32[7,16,128]{2,1,0:T(8,128)S(1)} collective-permute-done((f32[7,16,128]{2,1,0:T(8,128)S(1)}, f32[7,16,128]{2,1,0:T(8,128)S(1)}, u32[]{:S(2)}, u32[]{:S(2)}) %collective-permute-start.2) | collective-permute-done | bytes 57376 | tf_op jit(solution)/shard_map/ppermute | solution.py:421
  45.1 3.4 %collective-permute-done.3.second = f32[7,16,128]{2,1,0:T(8,128)S(1)} collective-permute-done((f32[7,16,128]{2,1,0:T(8,128)S(1)}, f32[7,16,128]{2,1,0:T(8,128)S(1)}, u32[]{:S(2)}, u32[]{:S(2)}) %collective-permute-start.3) | collective-permute-done | bytes 57376 | tf_op jit(solution)/shard_map/ppermute | solution.py:421
  48.5 3.8 %shard_map.115 = (f32[4,128,128]{2,1,0:T(8,128)S(1)}, f32[10,160,128]{2,1,0:T(8,128)S(1)}) custom-call(f32[4,128,128]{2,1,0:T(8,128)S(1)} %get-tuple-element.31.ctl, f32[2,128,128]{2,1,0:T(8,128)S(1)} %get-tuple-element.32.rate, f32[128,128]{1,0:T(8,128)S(1)} %get-tuple-element.35.strip, f32[7,16,128]{2,1,0:T(8,128)S(1)} %collective-permute-done.2.first, ...), custom_call_target="tpu_custom_call" | custom-call | flops 40000000 | bytes 1654784 | tf_op jit(solution)/shard_map/pallas_call | solution.py:49
  52.3 0.0 all-to-all-done.1.sent
  52.3 0.8 shard_map.117
  53.1 11.5 %all_to_all.33 = f32[8,32,128]{2,1,0:T(8,128)S(1)} all-to-all(f32[8,32,128]{2,1,0:T(8,128)S(1)} %bitcast.19), channel_id=1, replica_groups=mesh['gx'=8,'gy'=8,'obs'=8] {'obs'}, dimensions={0} | all-to-all | bytes 262144 | tf_op jit(solution)/shard_map/all_to_all | solution.py:425
  64.6 1.9 %shard_map.118 = (f32[4,128,128]{2,1,0:T(8,128)S(1)}, f32[128,128]{1,0:T(8,128)S(1)}, f32[128,128]{1,0:T(8,128)S(1)}, f32[64,4,128]{2,1,0:T(4,128)}) custom-call(f32[256,128]{1,0:T(8,128)S(1)} %bitcast.18, f32[136,128]{1,0:T(8,128)S(1)} %get-tuple-element.44.tab), custom_call_target="tpu_custom_call" | custom-call | flops 400000000 | bytes 724992 | tf_op jit(solution)/shard_map/pallas_call | solution.py:49
  66.5 9.9 %all-to-all-start.3 = ((f32[64,4,128]{2,1,0:T(4,128)}), f32[64,4,128]{2,1,0:T(4,128)S(1)}, u32[]{:S(2)}, u32[]{:S(2)}) async-start(f32[64,4,128]{2,1,0:T(4,128)} %get-tuple-element.52), calls=%async_computation.3 | async-start | bytes 262144 | tf_op jit(solution)/shard_map/all_to_all | solution.py:425
  76.4 0.1 collective-permute-start.4
  76.5 2.8 %collective-permute-start.5 = (f32[128,128]{1,0:T(8,128)S(1)}, f32[128,128]{1,0:T(8,128)S(1)}, u32[]{:S(2)}, u32[]{:S(2)}) collective-permute-start(f32[128,128]{1,0:T(8,128)S(1)} %get-tuple-element.47), channel_id=1, source_target_pairs={{0,448},{64,0},{128,64},{192,128},{256,192},{320,256},{384,320},{4... | collective-permute-start | bytes 196616 | tf_op jit(solution)/shard_map/ppermute | solution.py:413
  79.3 2.6 %collective-permute-done.4.left = f32[128,128]{1,0:T(8,128)S(1)} collective-permute-done((f32[128,128]{1,0:T(8,128)S(1)}, f32[128,128]{1,0:T(8,128)S(1)}, u32[]{:S(2)}, u32[]{:S(2)}) %collective-permute-start.4) | collective-permute-done | bytes 65568 | tf_op jit(solution)/shard_map/ppermute | solution.py:412
  81.9 0.0 collective-permute-done.5.right
  81.9 2.4 %collective-permute-start.6 = (f32[5,16,128]{2,1,0:T(8,128)S(1)}, f32[5,16,128]{2,1,0:T(8,128)S(1)}, u32[]{:S(2)}, u32[]{:S(2)}) collective-permute-start(f32[5,16,128]{2,1,0:T(8,128)S(1)} %get-tuple-element.49), channel_id=1, source_target_pairs={{0,8},{8,0},{16,24},{24,16},{32,40},{40,32},{48,56},{56,48},{1,9},... | collective-permute-start | bytes 122888 | tf_op jit(solution)/shard_map/ppermute | solution.py:421
  84.3 2.3 %collective-permute-start.7 = (f32[5,16,128]{2,1,0:T(8,128)S(1)}, f32[5,16,128]{2,1,0:T(8,128)S(1)}, u32[]{:S(2)}, u32[]{:S(2)}) collective-permute-start(f32[5,16,128]{2,1,0:T(8,128)S(1)} %get-tuple-element.50), channel_id=1, source_target_pairs={{8,16},{16,8},{24,32},{32,24},{40,48},{48,40},{9,17},{17,9},{25,33... | collective-permute-start | bytes 122888 | tf_op jit(solution)/shard_map/ppermute | solution.py:421
  86.6 1.2 %collective-permute-done.6.first = f32[5,16,128]{2,1,0:T(8,128)S(1)} collective-permute-done((f32[5,16,128]{2,1,0:T(8,128)S(1)}, f32[5,16,128]{2,1,0:T(8,128)S(1)}, u32[]{:S(2)}, u32[]{:S(2)}) %collective-permute-start.6) | collective-permute-done | bytes 40992 | tf_op jit(solution)/shard_map/ppermute | solution.py:421
  87.8 3.6 %collective-permute-done.7.second = f32[5,16,128]{2,1,0:T(8,128)S(1)} collective-permute-done((f32[5,16,128]{2,1,0:T(8,128)S(1)}, f32[5,16,128]{2,1,0:T(8,128)S(1)}, u32[]{:S(2)}, u32[]{:S(2)}) %collective-permute-start.7) | collective-permute-done | bytes 40992 | tf_op jit(solution)/shard_map/ppermute | solution.py:421
  91.5 4.3 %shard_map.120 = f32[4,128,128]{2,1,0:T(8,128)} custom-call(f32[4,128,128]{2,1,0:T(8,128)S(1)} %get-tuple-element.45.pulled, f32[128,128]{1,0:T(8,128)S(1)} %get-tuple-element.48.strip, f32[5,16,128]{2,1,0:T(8,128)S(1)} %collective-permute-done.6.first, f32[5,16,128]{2,1,0:T(8,128)S(1)} %collective-permute-done.7.second, ...), custom_call_target="tpu_custom_call" | custom-call | flops 40000000 | bytes 1753088 | tf_op jit(solution)/shard_map/pallas_call | solution.py:49
  95.8 0.0 all-to-all-done.3.columns
  95.8 1.4 %shard_map.121 = f32[4,128]{1,0:T(4,128)} custom-call(f32[64,4,128]{2,1,0:T(4,128)S(1)} %all-to-all-done.3.columns, s32[1,512]{1,0:T(1,128)S(1)} %get-tuple-element.40.holder, f32[1,512]{1,0:T(1,128)S(1)} %get-tuple-element.53.slots, s32[4,128]{1,0:T(4,128)S(1)} %get-tuple-element.54.prof, s32[4,128]{1,0:T(4,128)S(1)} %get-tuple-element.55.field, ...), custom_call_target="tpu_custom_call" | custom-call | flops 400000000 | bytes 149504 | tf_op jit(solution)/shard_map/pallas_call | solution.py:49
  (2 shorter events, 0.0 us)
Async XLA Ops:
  23.1 29.2 %all-to-all-start.1 = ((f32[64,1,384]{2,1,0:T(1,128)}), f32[64,1,384]{2,1,0:T(1,128)S(1)}, u32[]{:S(2)}, u32[]{:S(2)}) async-start(f32[64,1,384]{2,1,0:T(1,128)} %get-tuple-element.42), calls=%async_computation.1 | async-start | bytes 196608 | tf_op jit(solution)/shard_map/all_to_all | solution.py:425
  33.3 5.7 %collective-permute-start = (f32[128,128]{1,0:T(8,128)S(1)}, f32[128,128]{1,0:T(8,128)S(1)}, u32[]{:S(2)}, u32[]{:S(2)}) collective-permute-start(f32[128,128]{1,0:T(8,128)S(1)} %get-tuple-element.33), channel_id=1, source_target_pairs={{0,64},{64,128},{128,192},{192,256},{256,320},{320,384},{384,448},... | collective-permute-start | bytes 196616 | tf_op jit(solution)/shard_map/ppermute | solution.py:412
  33.4 5.5 %collective-permute-start.1 = (f32[128,128]{1,0:T(8,128)S(1)}, f32[128,128]{1,0:T(8,128)S(1)}, u32[]{:S(2)}, u32[]{:S(2)}) collective-permute-start(f32[128,128]{1,0:T(8,128)S(1)} %get-tuple-element.34), channel_id=1, source_target_pairs={{0,448},{64,0},{128,64},{192,128},{256,192},{320,256},{384,320},{4... | collective-permute-start | bytes 196616 | tf_op jit(solution)/shard_map/ppermute | solution.py:413
  39.0 6.1 %collective-permute-start.2 = (f32[7,16,128]{2,1,0:T(8,128)S(1)}, f32[7,16,128]{2,1,0:T(8,128)S(1)}, u32[]{:S(2)}, u32[]{:S(2)}) collective-permute-start(f32[7,16,128]{2,1,0:T(8,128)S(1)} %get-tuple-element.36), channel_id=1, source_target_pairs={{0,8},{8,0},{16,24},{24,16},{32,40},{40,32},{48,56},{56,48},{1,9},... | collective-permute-start | bytes 172040 | tf_op jit(solution)/shard_map/ppermute | solution.py:421
  41.2 7.3 %collective-permute-start.3 = (f32[7,16,128]{2,1,0:T(8,128)S(1)}, f32[7,16,128]{2,1,0:T(8,128)S(1)}, u32[]{:S(2)}, u32[]{:S(2)}) collective-permute-start(f32[7,16,128]{2,1,0:T(8,128)S(1)} %get-tuple-element.37), channel_id=1, source_target_pairs={{8,16},{16,8},{24,32},{32,24},{40,48},{48,40},{9,17},{17,9},{25,33... | collective-permute-start | bytes 172040 | tf_op jit(solution)/shard_map/ppermute | solution.py:421
  66.5 29.3 %all-to-all-start.3 = ((f32[64,4,128]{2,1,0:T(4,128)}), f32[64,4,128]{2,1,0:T(4,128)S(1)}, u32[]{:S(2)}, u32[]{:S(2)}) async-start(f32[64,4,128]{2,1,0:T(4,128)} %get-tuple-element.52), calls=%async_computation.3 | async-start | bytes 262144 | tf_op jit(solution)/shard_map/all_to_all | solution.py:425
  76.4 5.5 %collective-permute-start.4 = (f32[128,128]{1,0:T(8,128)S(1)}, f32[128,128]{1,0:T(8,128)S(1)}, u32[]{:S(2)}, u32[]{:S(2)}) collective-permute-start(f32[128,128]{1,0:T(8,128)S(1)} %get-tuple-element.46), channel_id=1, source_target_pairs={{0,64},{64,128},{128,192},{192,256},{256,320},{320,384},{384,448},... | collective-permute-start | bytes 196616 | tf_op jit(solution)/shard_map/ppermute | solution.py:412
  76.5 5.4 %collective-permute-start.5 = (f32[128,128]{1,0:T(8,128)S(1)}, f32[128,128]{1,0:T(8,128)S(1)}, u32[]{:S(2)}, u32[]{:S(2)}) collective-permute-start(f32[128,128]{1,0:T(8,128)S(1)} %get-tuple-element.47), channel_id=1, source_target_pairs={{0,448},{64,0},{128,64},{192,128},{256,192},{320,256},{384,320},{4... | collective-permute-start | bytes 196616 | tf_op jit(solution)/shard_map/ppermute | solution.py:413
  81.9 5.9 %collective-permute-start.6 = (f32[5,16,128]{2,1,0:T(8,128)S(1)}, f32[5,16,128]{2,1,0:T(8,128)S(1)}, u32[]{:S(2)}, u32[]{:S(2)}) collective-permute-start(f32[5,16,128]{2,1,0:T(8,128)S(1)} %get-tuple-element.49), channel_id=1, source_target_pairs={{0,8},{8,0},{16,24},{24,16},{32,40},{40,32},{48,56},{56,48},{1,9},... | collective-permute-start | bytes 122888 | tf_op jit(solution)/shard_map/ppermute | solution.py:421
  84.3 7.1 %collective-permute-start.7 = (f32[5,16,128]{2,1,0:T(8,128)S(1)}, f32[5,16,128]{2,1,0:T(8,128)S(1)}, u32[]{:S(2)}, u32[]{:S(2)}) collective-permute-start(f32[5,16,128]{2,1,0:T(8,128)S(1)} %get-tuple-element.50), channel_id=1, source_target_pairs={{8,16},{16,8},{24,32},{32,24},{40,48},{48,40},{9,17},{17,9},{25,33... | collective-permute-start | bytes 122888 | tf_op jit(solution)/shard_map/ppermute | solution.py:421
